TPU v7x, 32 devices: a whole 2x2x4 slice. The times are simulated.
32 devices in a mesh: pop: 8 (over z, x), grp: 4 (over y, core).
Axes of the slice: x: 2, y: 2, z: 4, core: 2. Of those that a mesh axis runs over, the one named last changes fastest.
Arguments:
- actions: bfloat16 [16384, 1024], P(('pop', 'grp')), may hold values from -6 to 6
- elite_mask: int32 [16384], P(('pop', 'grp')), may hold values from 0 to 1, as said below
- init_state: float32 [256], replicated, may hold values from -6 to 6
- w_state: bfloat16 [256, 256], replicated, may hold values from -0.375 to 0.375
- w_action: bfloat16 [32, 256], replicated, may hold values from -1 to 1
- bias: float32 [256], replicated, may hold values from -3 to 3
- w_out: bfloat16 [256, 256], replicated, may hold values from -0.375 to 0.375
- reward_vec: float32 [256], replicated, may hold values from -0.375 to 0.375
Outputs:
- new_mean: float32 [1024], replicated
- covariance: float32 [1024, 1024], P('pop')
- returns: float32 [16384], P(('pop', 'grp'))
Inputs may be any that keep to these rules, and one draw needn't show every extreme that they name: `elite_mask`: each aligned block of 512 candidates (the candidates of one device) holds at least one elite.
All inputs are finite; a program needn't handle non-finite values.
Results may differ from a plain program's by a relative error of at most 0.0063.
Values sent between devices are 32-bit elements; how exact they have to be, the bound alone decides.
No kernel may reach another device: no remote copies, remote signals or barrier semaphores. Data moves between devices by JAX's collectives and lax.ppermute only.
A program may use at most 64 MiB of HBM per device.

v0:
```python
import jax
import jax.numpy as jnp
from jax import lax
from jax.sharding import PartitionSpec as P

ACT = 32
STEPS = 32
STATE = 256


def on_device(actions, elite_mask, init_state, w_state, w_action, bias, w_out, reward_vec):
    cand_rows = actions.shape[0]
    width_all = actions.shape[1]
    weight = elite_mask.astype(jnp.float32)
    weight_b = weight.astype(jnp.bfloat16)
    local_sums = jnp.dot(weight_b[None, :], actions, preferred_element_type=jnp.float32)[0]
    local_count = jnp.sum(weight)
    sums, count = lax.psum((local_sums, local_count), ("pop", "grp"))
    new_mean = sums / count
    masked = actions * weight_b[:, None]
    pop_count = lax.axis_size("pop")
    own_rows = width_all // pop_count
    pop_index = lax.axis_index("pop")
    first_row = pop_index * own_rows
    slab = lax.psum_scatter(
        lax.dot_general(
            masked, actions, (((0,), (0,)), ((), ())), preferred_element_type=jnp.float32
        ),
        "pop",
        scatter_dimension=0,
        tiled=True,
    )
    mine = lax.psum(slab, "grp")
    mean_rows = lax.dynamic_slice_in_dim(new_mean, first_row, own_rows, 0)
    covariance = mine / count - mean_rows[:, None] * new_mean[None, :]
    per_step = jnp.transpose(actions.reshape(cand_rows, STEPS, ACT), (1, 0, 2))
    start_state = jnp.broadcast_to(init_state[None, :], (cand_rows, STATE))

    def advance(carry, action_now):
        state, total = carry
        state_b = state.astype(jnp.bfloat16)
        pre = jnp.dot(state_b, w_state, preferred_element_type=jnp.float32)
        pre = pre + jnp.dot(action_now, w_action, preferred_element_type=jnp.float32) + bias
        hidden = jnp.tanh(pre).astype(jnp.bfloat16)
        state = 0.9 * state + jnp.dot(hidden, w_out, preferred_element_type=jnp.float32)
        total = total + jnp.sum(state * reward_vec[None, :], axis=1)
        return ((state, total), None)

    (final_state, total), unused = lax.scan(
        advance, (start_state, jnp.zeros((cand_rows,), jnp.float32)), per_step
    )
    returns = total / STEPS
    return (new_mean, covariance, returns)


def solution(mesh):
    placed = (P(("pop", "grp"), None), P(("pop", "grp")), P(), P(), P(), P(), P(), P())
    return jax.shard_map(
        on_device,
        mesh=mesh,
        in_specs=placed,
        out_specs=(P(), P("pop", None), P(("pop", "grp"))),
        check_vma=False,
    )
```

profile of v0, /device:TPU:0, one launch (start us, length us, event | category | flops | bytes accessed | tf_op | source)
XLA Modules:
  0.0 149.3 jit_solution(13293157726745126717)
XLA Ops:
  7.2 0.7 convert_convert_fusion
  7.9 5.0 %fusion.12 = f32[1024,1024]{1,0:T(8,128)} fusion(bf16[512,1024]{1,0:T(8,128)(2,1)} %param.10, bf16[512]{0:T(512)(128)(2,1)S(1)} %convert_convert_fusion), kind=kOutput, calls=%fused_computation.13 | convolution fusion | flops 1074266112 | bytes 5243904 | tf_op jit(solution)/shard_map/dot_general | solution.py:26
  13.0 0.5 copy.11
  13.9 34.1 %while.13 = (s32[]{:T(128)}, f32[512,256]{0,1:T(8,128)S(1)}, f32[512]{0:T(512)S(1)}, bf16[256,256]{1,0:T(8,128)(2,1)S(1)}, bf16[32,512,32]{1,2,0:T(8,128)(2,1)S(...) while((s32[]{:T(128)}, f32[512,256]{0,1:T(8,128)S(1)}, ...), condition=%wide.region_7.8_spmd.clone, body=%wide.region_5.7_spmd.clone.sunk | while | flops 143655424 | bytes 2943107 | solution.py:49
  13.9 0.3 fusion.35
  14.1 0.8 multiply_reduce_fusion.2
  15.2 0.8 multiply_reduce_fusion.2
  16.3 0.8 multiply_reduce_fusion.2
  17.3 0.8 multiply_reduce_fusion.2
  18.1 0.3 fusion.35
  18.4 0.8 multiply_reduce_fusion.2
  19.2 0.3 fusion.35
  19.5 0.8 multiply_reduce_fusion.2
  20.3 0.3 fusion.35
  20.5 0.8 multiply_reduce_fusion.2
  21.6 0.8 multiply_reduce_fusion.2
  22.7 0.8 multiply_reduce_fusion.2
  23.7 0.8 multiply_reduce_fusion.2
  24.5 0.3 fusion.35
  24.8 0.8 multiply_reduce_fusion.2
  25.9 0.8 multiply_reduce_fusion.2
  26.9 0.8 multiply_reduce_fusion.2
  28.0 0.8 multiply_reduce_fusion.2
  29.1 0.8 multiply_reduce_fusion.2
  30.1 0.8 multiply_reduce_fusion.2
  31.2 0.8 multiply_reduce_fusion.2
  32.2 0.8 multiply_reduce_fusion.2
  33.3 0.8 multiply_reduce_fusion.2
  34.4 0.8 multiply_reduce_fusion.2
  35.4 0.8 multiply_reduce_fusion.2
  36.5 0.8 multiply_reduce_fusion.2
  37.6 0.8 multiply_reduce_fusion.2
  38.6 0.8 multiply_reduce_fusion.2
  39.7 0.8 multiply_reduce_fusion.2
  40.8 0.8 multiply_reduce_fusion.2
  41.8 0.8 multiply_reduce_fusion.2
  42.9 0.8 multiply_reduce_fusion.2
  44.0 0.8 multiply_reduce_fusion.2
  45.0 0.8 multiply_reduce_fusion.2
  46.1 0.8 multiply_reduce_fusion.2
  47.2 0.8 multiply_reduce_fusion.2
  48.0 0.6 convert_reduce_fusion
  48.8 42.3 %all-reduce = (f32[1024]{0:T(1024)S(1)}, f32[]{:T(128)}) all-reduce(f32[1024]{0:T(1024)S(1)} %bitcast.26, f32[]{:T(128)} %convert_reduce_fusion), channel_id=1, replica_groups=mesh['pop'=8,'grp'=4] {'pop','grp'}, use_global_device_ids=true, to_apply=%region_0.0 | all-reduce | flops 1025 | bytes 8200 | tf_op jit(solution)/shard_map/psum | solution.py:18
  91.1 13.3 %reduce-scatter.2.cloned.1.call-done = f32[128,1024]{1,0:T(8,128)} async-done(((f32[1024,1024]{1,0:T(8,128)}), f32[128,1024]{1,0:T(8,128)}) %reduce-scatter.2.cloned.1.call-update) | async-done | bytes 524304 | tf_op jit(solution)/shard_map/reduce_scatter | solution.py:25
  104.5 0.6 broadcast_divide_fusion
  105.2 0.6 broadcast_multiply_fusion
  105.8 34.1 %all-reduce.3.cloned.1.call-done = f32[128,1024]{1,0:T(8,128)} async-done(((f32[128,1024]{1,0:T(8,128)}), f32[128,1024]{1,0:T(8,128)}) %all-reduce.3.cloned.1.call-update) | async-done | bytes 524304 | tf_op jit(solution)/shard_map/psum | solution.py:33
  139.9 2.6 %multiply_subtract_fusion = f32[128,1024]{1,0:T(8,128)} fusion(f32[128,1024]{1,0:T(8,128)} %all-reduce.3.cloned.1.call-done, f32[1024]{0:T(1024)S(1)} %broadcast_divide_fusion, f32[128]{0:T(128)S(1)} %dynamic_slice.7, f32[]{:T(128)} %get-tuple-element.109), kind=kLoop, calls=%fused_computation.15 | loop fusion | flops 393216 | bytes 1053188 | tf_op jit(solution)/shard_map/sub | solution.py:35
  (86 shorter events, 8.3 us)
Async XLA Ops:
  7.2 97.3 %reduce-scatter.2.cloned.1.call-start = ((), (), s32[]{:S(2)}) async-start(), calls=%async_computation.1 | async-start | bytes 4718592 | tf_op jit(solution)/shard_map/reduce_scatter | solution.py:25
  7.9 5.1 %copy-start = (bf16[512,1024]{1,0:T(8,128)(2,1)S(1)}, bf16[512,1024]{1,0:T(8,128)(2,1)}, u32[]{:S(2)}) copy-start(bf16[512,1024]{1,0:T(8,128)(2,1)} %param.10) | copy-start | bytes 3145732
  12.9 0.7 copy-start.8
  12.9 0.9 copy-start.1
  12.9 1.0 copy-start.2
  12.9 1.0 copy-start.3
  12.9 1.0 copy-start.4
  12.9 1.0 copy-start.5
  12.9 127.0 %all-reduce.3.cloned.1.call-start = ((), (), s32[]{:S(2)}) async-start(), calls=%async_computation.2 | async-start | bytes 1048576 | tf_op jit(solution)/shard_map/psum | solution.py:33
  13.9 34.1 %copy-start.7 = (s32[512]{0:T(512)S(1)}, s32[512]{0:T(512)}, u32[]{:S(2)}) copy-start(s32[512]{0:T(512)} %param.11) | copy-start | bytes 6148
  105.1 37.3 %copy-start.6 = (f32[1024]{0:T(1024)}, f32[1024]{0:T(1024)S(1)}, u32[]{:S(2)}) copy-start(f32[1024]{0:T(1024)S(1)} %broadcast_divide_fusion) | copy-start | bytes 12292
Sparse Core Ops, SparseCore 0:
  13.0 91.3 reduce-scatter.1
  106.8 33.0 all-reduce.2
where the time goes:
time: 150 us; the launch traced here: 149 us
  waiting for transfers between devices  47.5 us (32%)
  blocking collectives  42.3 us (28%)
  matrix products  38.2 us (25%)
  between operations  14.2 us (9%)
  other arithmetic  5.48 us (4%)
    psum x1, blocking collectives, on_device(): sums, count = lax.psum((local_sums, local_count), ('pop', 'grp'))  42.3 us
    psum x1, waiting for transfers between devices, on_device(): mine = lax.psum(slab, 'grp')  34.1 us
    dot_general x32, matrix products, advance(): jnp.dot(hidden, w_out, preferred_element_type=jnp.float32)  24.6 us
    reduce_scatter x1, waiting for transfers between devices, on_device(): lax.psum_scatter(lax.dot_general(masked, actions, (((0,), (0,)), ((), ())...  13.3 us
    dot_general x32, matrix products, advance(): pre = jnp.dot(state_b, w_state, preferred_element_type=jnp.float32)  8.45 us
    dot_general x1, matrix products, on_device(): lax.dot_general(masked, actions, (((0,), (0,)), ((), ())), preferred_elem...  4.96 us
  transfers between devices with their start and end apart: 2, of which 2 were waited for; matrix products, arithmetic and copies ran while one was open for 24% of the time, Pallas kernels for 0%

commit v1 on v0

--- a/solution.py
+++ b/solution.py
@@ -30,7 +30,9 @@
         scatter_dimension=0,
         tiled=True,
     )
-    mine = lax.psum(slab, "grp")
+    mine = slab
+    for hop in (1, 2):
+        mine = mine + lax.ppermute(mine, "grp", [(dev, dev ^ hop) for dev in range(4)])
     mean_rows = lax.dynamic_slice_in_dim(new_mean, first_row, own_rows, 0)
     covariance = mine / count - mean_rows[:, None] * new_mean[None, :]
     per_step = jnp.transpose(actions.reshape(cand_rows, STEPS, ACT), (1, 0, 2))

time: 150 us -> 197 us (1.31)
  waiting for transfers between devices: 47.5 us -> 90.7 us
  blocking collectives: 42.3 us -> 45.2 us
    reduce_scatter x1, waiting for transfers between devices: 13.3 us -> 90.6 us  [on_device(): lax.psum_scatter(lax.dot_general(masked, actions, (((0,), (0,)), ((), ())...]
    psum x1 -> x0, waiting for transfers between devices: 34.1 us -> none  [on_device(): mine = lax.psum(slab, 'grp')]
    psum x1, blocking collectives: 42.3 us -> 45.2 us  [on_device(): sums, count = lax.psum((local_sums, local_count), ('pop', 'grp'))]
  transfers between devices with their start and end apart: 2 -> 3, of which waited for: 2 -> 1; matrix products, arithmetic and copies ran while one was open for 24% -> 18% of each run, Pallas kernels for 0% -> 0%
where the time goes in v1:
time: 197 us
  waiting for transfers between devices  90.7 us (46%)
  blocking collectives  45.2 us (23%)
  matrix products  38.2 us (19%)
  between operations  14.2 us (7%)
  other arithmetic  5.56 us (3%)
    reduce_scatter x1, waiting for transfers between devices, on_device(): lax.psum_scatter(lax.dot_general(masked, actions, (((0,), (0,)), ((), ())...  90.6 us
    psum x1, blocking collectives, on_device(): sums, count = lax.psum((local_sums, local_count), ('pop', 'grp'))  45.2 us
    dot_general x32, matrix products, advance(): jnp.dot(hidden, w_out, preferred_element_type=jnp.float32)  24.6 us
    dot_general x32, matrix products, advance(): pre = jnp.dot(state_b, w_state, preferred_element_type=jnp.float32)  8.45 us
    dot_general x1, matrix products, on_device(): lax.dot_general(masked, actions, (((0,), (0,)), ((), ())), preferred_elem...  4.95 us
  transfers between devices with their start and end apart: 3, of which 1 were waited for; matrix products, arithmetic and copies ran while one was open for 18% of the time, Pallas kernels for 0%

profile of v1, /device:TPU:0, one launch (start us, length us, event | category | flops | bytes accessed | tf_op | source)
XLA Modules:
  0.0 196.8 jit_solution(16101372539195447534)
XLA Ops:
  7.2 0.7 convert_convert_fusion
  7.9 4.9 %fusion.12 = f32[1024,1024]{1,0:T(8,128)} fusion(bf16[512,1024]{1,0:T(8,128)(2,1)} %param.10, bf16[512]{0:T(512)(128)(2,1)S(1)} %convert_convert_fusion), kind=kOutput, calls=%fused_computation.13 | convolution fusion | flops 1074266112 | bytes 5243904 | tf_op jit(solution)/shard_map/dot_general | solution.py:26
  12.9 0.5 copy.11
  13.5 90.6 %reduce-scatter.2.cloned.1.call-done = f32[128,1024]{1,0:T(8,128)} async-done(((f32[1024,1024]{1,0:T(8,128)}), f32[128,1024]{1,0:T(8,128)}) %reduce-scatter.2.cloned.1.call-update) | async-done | bytes 524304 | tf_op jit(solution)/shard_map/reduce_scatter | solution.py:25
  104.3 34.1 %while.13 = (s32[]{:T(128)}, f32[512,256]{0,1:T(8,128)S(1)}, f32[512]{0:T(512)S(1)}, bf16[256,256]{1,0:T(8,128)(2,1)S(1)}, bf16[32,512,32]{1,2,0:T(8,128)(2,1)S(...) while((s32[]{:T(128)}, f32[512,256]{0,1:T(8,128)S(1)}, ...), condition=%wide.region_6.7_spmd.clone, body=%wide.region_4.6_spmd.clone.sunk | while | flops 143655424 | bytes 2943107 | solution.py:51
  104.6 0.8 multiply_reduce_fusion.2
  105.4 0.3 fusion.35
  105.6 0.8 multiply_reduce_fusion.2
  106.4 0.3 fusion.35
  106.7 0.8 multiply_reduce_fusion.2
  107.5 0.3 fusion.35
  107.8 0.8 multiply_reduce_fusion.2
  108.8 0.8 multiply_reduce_fusion.2
  109.9 0.8 multiply_reduce_fusion.2
  111.0 0.8 multiply_reduce_fusion.2
  111.8 0.3 fusion.35
  112.0 0.8 multiply_reduce_fusion.2
  113.1 0.8 multiply_reduce_fusion.2
  114.2 0.8 multiply_reduce_fusion.2
  115.2 0.8 multiply_reduce_fusion.2
  116.3 0.8 multiply_reduce_fusion.2
  117.4 0.8 multiply_reduce_fusion.2
  118.4 0.8 multiply_reduce_fusion.2
  119.5 0.8 multiply_reduce_fusion.2
  120.6 0.8 multiply_reduce_fusion.2
  121.6 0.8 multiply_reduce_fusion.2
  122.7 0.8 multiply_reduce_fusion.2
  123.7 0.8 multiply_reduce_fusion.2
  124.8 0.8 multiply_reduce_fusion.2
  125.9 0.8 multiply_reduce_fusion.2
  126.9 0.8 multiply_reduce_fusion.2
  128.0 0.8 multiply_reduce_fusion.2
  129.1 0.8 multiply_reduce_fusion.2
  130.1 0.8 multiply_reduce_fusion.2
  131.2 0.8 multiply_reduce_fusion.2
  132.3 0.8 multiply_reduce_fusion.2
  133.3 0.8 multiply_reduce_fusion.2
  134.4 0.8 multiply_reduce_fusion.2
  135.5 0.8 multiply_reduce_fusion.2
  136.5 0.8 multiply_reduce_fusion.2
  137.6 0.8 multiply_reduce_fusion.2
  138.7 1.3 add.35
  139.9 1.5 collective-permute-start.1
  141.5 0.6 convert_reduce_fusion
  142.1 45.2 %all-reduce = (f32[1024]{0:T(1024)S(1)}, f32[]{:T(128)}) all-reduce(f32[1024]{0:T(1024)S(1)} %bitcast.26, f32[]{:T(128)} %convert_reduce_fusion), channel_id=1, replica_groups=mesh['pop'=8,'grp'=4] {'pop','grp'}, use_global_device_ids=true, to_apply=%region_0.0 | all-reduce | flops 1025 | bytes 8200 | tf_op jit(solution)/shard_map/psum | solution.py:18
  187.2 0.6 broadcast_divide_fusion
  187.9 0.6 broadcast_multiply_fusion
  188.5 1.5 multiply_subtract_fusion
  (88 shorter events, 8.3 us)
Async XLA Ops:
  7.2 97.0 %reduce-scatter.2.cloned.1.call-start = ((), (), s32[]{:S(2)}) async-start(), calls=%async_computation.1 | async-start | bytes 4718592 | tf_op jit(solution)/shard_map/reduce_scatter | solution.py:25
  7.9 5.0 %copy-start = (bf16[512,1024]{1,0:T(8,128)(2,1)S(1)}, bf16[512,1024]{1,0:T(8,128)(2,1)}, u32[]{:S(2)}) copy-start(bf16[512,1024]{1,0:T(8,128)(2,1)} %param.10) | copy-start | bytes 3145732
  12.8 91.3 %copy-start.8 = (f32[256]{0:T(256)S(1)}, f32[256]{0:T(256)}, u32[]{:S(2)}) copy-start(f32[256]{0:T(256)} %param.12) | copy-start | bytes 3076
  12.9 91.4 %copy-start.1 = (bf16[256,256]{1,0:T(8,128)(2,1)S(1)}, bf16[256,256]{1,0:T(8,128)(2,1)}, u32[]{:S(2)}) copy-start(bf16[256,256]{1,0:T(8,128)(2,1)} %param.13) | copy-start | bytes 393220
  12.9 91.4 %copy-start.2 = (bf16[256,256]{1,0:T(8,128)(2,1)S(1)}, bf16[256,256]{1,0:T(8,128)(2,1)}, u32[]{:S(2)}) copy-start(bf16[256,256]{1,0:T(8,128)(2,1)} %param.16) | copy-start | bytes 393220
  12.9 91.4 %copy-start.3 = (bf16[32,256]{1,0:T(8,128)(2,1)S(1)}, bf16[32,256]{1,0:T(8,128)(2,1)}, u32[]{:S(2)}) copy-start(bf16[32,256]{1,0:T(8,128)(2,1)} %param.14) | copy-start | bytes 49156
  12.9 91.4 %copy-start.4 = (f32[256]{0:T(256)S(1)}, f32[256]{0:T(256)}, u32[]{:S(2)}) copy-start(f32[256]{0:T(256)} %param.15) | copy-start | bytes 3076
  12.9 91.4 %copy-start.5 = (f32[256]{0:T(256)S(1)}, f32[256]{0:T(256)}, u32[]{:S(2)}) copy-start(f32[256]{0:T(256)} %param.17) | copy-start | bytes 3076
  104.1 34.5 %collective-permute-start = (f32[128,1024]{1,0:T(8,128)}, f32[128,1024]{1,0:T(8,128)}, u32[]{:S(2)}, u32[]{:S(2)}) collective-permute-start(f32[128,1024]{1,0:T(8,128)} %reduce-scatter.2.cloned.1.call-done), channel_id=1, source_target_pairs={{0,1},{1,0},{2,3},{3,2},{4,5},{5,4},{6,7},{7,6},{8,9},{9,8},{10,11... | collective-permute-start | bytes 1572872 | tf_op jit(solution)/shard_map/ppermute | solution.py:35
  104.3 37.2 %copy-start.7 = (s32[512]{0:T(512)S(1)}, s32[512]{0:T(512)}, u32[]{:S(2)}) copy-start(s32[512]{0:T(512)} %param.11) | copy-start | bytes 6148
  139.9 48.6 %collective-permute-start.1 = (f32[128,1024]{1,0:T(8,128)S(1)}, f32[128,1024]{1,0:T(8,128)S(1)}, u32[]{:S(2)}, u32[]{:S(2)}) collective-permute-start(f32[128,1024]{1,0:T(8,128)S(1)} %add.35), channel_id=1, source_target_pairs={{0,2},{1,3},{2,0},{3,1},{4,6},{5,7},{6,4},{7,5},{8,10},{9,11},{10,... | collective-permute-start | bytes 1572872 | tf_op jit(solution)/shard_map/ppermute | solution.py:35
  187.8 2.1 %copy-start.6 = (f32[1024]{0:T(1024)}, f32[1024]{0:T(1024)S(1)}, u32[]{:S(2)}) copy-start(f32[1024]{0:T(1024)S(1)} %broadcast_divide_fusion) | copy-start | bytes 12292
Sparse Core Ops, SparseCore 0:
  13.0 91.0 reduce-scatter.1
